TPU v7x, 32 devices: a whole 2x2x4 slice. The times are simulated.
32 devices in a mesh: fsdp: 8 (over z, y), tensor: 4 (over x, core).
Axes of the slice: x: 2, y: 2, z: 4, core: 2. Of those that a mesh axis runs over, the one named last changes fastest.
Arguments:
- tokens: bfloat16 [64, 1024, 1024], P('fsdp', 'tensor'), may hold values from -6 to 6
- cotangent: bfloat16 [64, 1024, 1024], P('fsdp', 'tensor'), may hold values from -6 to 6
- routed_index: int32 [64, 128], P('fsdp'), may hold values from 0 to 1023, as said below
- query_weight: bfloat16 [1024, 1024], P('fsdp', 'tensor'), may hold values from -0.1875 to 0.1875
- key_weight: bfloat16 [1024, 1024], P('fsdp', 'tensor'), may hold values from -0.1875 to 0.1875
- value_weight: bfloat16 [1024, 1024], P('fsdp', 'tensor'), may hold values from -0.1875 to 0.1875
- output_weight: bfloat16 [1024, 1024], P('tensor', 'fsdp'), may hold values from -0.5 to 0.5
- up_weight: bfloat16 [1024, 4096], P('fsdp', 'tensor'), may hold values from -0.1875 to 0.1875
- down_weight: bfloat16 [4096, 1024], P('tensor', 'fsdp'), may hold values from -0.09375 to 0.09375
- router_weight: bfloat16 [1024], P('fsdp'), may hold values from -0.1875 to 0.1875
- attn_gain: bfloat16 [1024], P('fsdp'), may hold values from 0.5 to 1.5
- mlp_gain: bfloat16 [1024], P('fsdp'), may hold values from 0.5 to 1.5
Outputs:
- mixed: bfloat16 [64, 1024, 1024], P('fsdp', 'tensor')
- token_grad: bfloat16 [64, 1024, 1024], P('fsdp', 'tensor')
- query_weight_grad: float32 [1024, 1024], P('fsdp', 'tensor')
- key_weight_grad: float32 [1024, 1024], P('fsdp', 'tensor')
- value_weight_grad: float32 [1024, 1024], P('fsdp', 'tensor')
- output_weight_grad: float32 [1024, 1024], P('tensor', 'fsdp')
- up_weight_grad: float32 [1024, 4096], P('fsdp', 'tensor')
- down_weight_grad: float32 [4096, 1024], P('tensor', 'fsdp')
- router_weight_grad: float32 [1024], P('fsdp')
- attn_gain_grad: float32 [1024], P('fsdp')
- mlp_gain_grad: float32 [1024], P('fsdp')
Inputs may be any that keep to these rules, and one draw needn't show every extreme that they name: `routed_index`: each row holds 128 distinct positions of one sequence in ascending order; its first is 0 and its last is 1023.
All inputs are finite; a program needn't handle non-finite values.
Results may differ from a plain program's by a relative error of at most 0.011.
Values may be sent and summed in bfloat16 or wider, within the bound.
No kernel may reach another device: no remote copies, remote signals or barrier semaphores. Data moves between devices by JAX's collectives and lax.ppermute only.
A program may use at most 192 MiB of HBM per device.

v0:
```python
import jax
import jax.numpy as jnp
from jax import lax
from jax.sharding import PartitionSpec as P

HEAD_DIM = 64
BLOCK = 256
EPS = 1e-06
NEG = -1e30
HIGH = lax.Precision.HIGHEST


def pick_rows(values, routed_index, offset, pos_span):
    local_pos = routed_index - offset
    inside = (local_pos >= 0) & (local_pos < pos_span)
    safe_pos = jnp.clip(local_pos, 0, pos_span - 1)
    chosen = jnp.take_along_axis(values, safe_pos[:, :, None], axis=1).astype(jnp.float32)
    return jnp.where(inside[:, :, None], chosen, jnp.zeros_like(chosen))


def place_target(routed_index, offset, pos_span):
    local_pos = routed_index - offset
    inside = (local_pos >= 0) & (local_pos < pos_span)
    return jnp.where(inside, local_pos, pos_span)


def place_rows(values, new_rows, target):
    seq_ids = jnp.arange(values.shape[0], dtype=jnp.int32)[:, None]
    return values.at[seq_ids, target].set(new_rows, mode="drop")


def rms_scale(inputs):
    return lax.rsqrt(jnp.mean(inputs * inputs, axis=-1, keepdims=True) + EPS)


def norm_back(grad_out, inputs, scale_rows, gain):
    normal = inputs * scale_rows
    grad_norm = grad_out * gain
    grad_in = scale_rows * (
        grad_norm - normal * jnp.mean(grad_norm * normal, axis=-1, keepdims=True)
    )
    return (grad_in, jnp.sum(grad_out * normal, axis=0))


def attend_scores(query_heads, key_heads, allowed, score_scale):
    scores = (
        jnp.einsum("sqhe,skhe->shqk", query_heads, key_heads, preferred_element_type=jnp.float32)
        * score_scale
    )
    return jnp.where(allowed[:, None], scores, NEG)


def shards(
    tokens,
    cotangent,
    routed_index,
    query_weight,
    key_weight,
    value_weight,
    output_weight,
    up_weight,
    down_weight,
    router_weight,
    attn_gain,
    mlp_gain,
):
    tensor_count = lax.axis_size("tensor")
    tensor_rank = lax.axis_index("tensor")
    seq_count, pos_span, model_width = tokens.shape
    routed = routed_index.shape[1]
    share_rows = routed // tensor_count
    offset = tensor_rank * pos_span
    score_scale = HEAD_DIM ** (-0.5)
    strided = (seq_count, share_rows, tensor_count, model_width)
    mine = (seq_count, share_rows, 1, model_width)
    picked_tokens = pick_rows(tokens, routed_index, offset, pos_span).reshape(strided)
    picked_grads = pick_rows(cotangent, routed_index, offset, pos_span).reshape(strided)
    token_share, grad_share = (
        lax.psum_scatter(
            picked_tokens.astype(jnp.bfloat16), "tensor", scatter_dimension=2, tiled=True
        ).astype(jnp.float32),
        lax.psum_scatter(
            picked_grads.astype(jnp.bfloat16), "tensor", scatter_dimension=2, tiled=True
        ).astype(jnp.float32),
    )
    flat_tokens = token_share.reshape(-1, model_width)
    grad_flat = grad_share.reshape(-1, model_width)
    full_params = (
        lax.all_gather(query_weight, "fsdp", axis=0, tiled=True),
        lax.all_gather(key_weight, "fsdp", axis=0, tiled=True),
        lax.all_gather(value_weight, "fsdp", axis=0, tiled=True),
        lax.all_gather(output_weight, "fsdp", axis=1, tiled=True),
        lax.all_gather(up_weight, "fsdp", axis=0, tiled=True),
        lax.all_gather(down_weight, "fsdp", axis=1, tiled=True),
        lax.all_gather(router_weight, "fsdp", axis=0, tiled=True),
        lax.all_gather(attn_gain, "fsdp", axis=0, tiled=True),
        lax.all_gather(mlp_gain, "fsdp", axis=0, tiled=True),
    )
    (
        query_full,
        key_full,
        value_full,
        output_full,
        up_full,
        down_full,
        router_full,
        first_gain,
        second_gain,
    ) = full_params
    router_logit = jnp.dot(flat_tokens, router_full.astype(jnp.float32), precision=HIGH)
    gate_value = jax.nn.sigmoid(router_logit)
    first_scale = rms_scale(flat_tokens)
    first_normed = (flat_tokens * first_scale * first_gain.astype(jnp.float32)).astype(jnp.bfloat16)
    normed_all = lax.all_gather(first_normed.reshape(mine), "tensor", axis=2, tiled=True).reshape(
        -1, model_width
    )
    local_width = query_full.shape[1]
    heads_local = local_width // HEAD_DIM
    head_shape = (seq_count, routed, heads_local, HEAD_DIM)
    query_heads = (
        jnp.dot(normed_all, query_full, preferred_element_type=jnp.float32)
        .astype(jnp.bfloat16)
        .reshape(head_shape)
    )
    key_heads = (
        jnp.dot(normed_all, key_full, preferred_element_type=jnp.float32)
        .astype(jnp.bfloat16)
        .reshape(head_shape)
    )
    value_heads = (
        jnp.dot(normed_all, value_full, preferred_element_type=jnp.float32)
        .astype(jnp.bfloat16)
        .reshape(head_shape)
    )
    blocks = routed_index // BLOCK
    allowed = blocks[:, None, :] <= blocks[:, :, None]
    scores = attend_scores(query_heads, key_heads, allowed, score_scale)
    top_score = jnp.max(scores, axis=-1, keepdims=True)
    log_total = top_score + jnp.log(jnp.sum(jnp.exp(scores - top_score), axis=-1, keepdims=True))
    attn_probs = jnp.exp(scores - log_total).astype(jnp.bfloat16)
    context = (
        jnp.einsum("shqk,skhe->sqhe", attn_probs, value_heads, preferred_element_type=jnp.float32)
        .astype(jnp.bfloat16)
        .reshape(-1, local_width)
    )
    attn_part = jnp.dot(context, output_full, preferred_element_type=jnp.float32)
    attn_share = lax.psum_scatter(
        attn_part.reshape(strided), "tensor", scatter_dimension=2, tiled=True
    ).reshape(-1, model_width)
    hidden_in = flat_tokens + attn_share
    second_scale = rms_scale(hidden_in)
    second_gain_f = second_gain.astype(jnp.float32)
    second_normed = (hidden_in * second_scale * second_gain_f).astype(jnp.bfloat16)
    normed_mid = lax.all_gather(second_normed.reshape(mine), "tensor", axis=2, tiled=True).reshape(
        -1, model_width
    )
    up_value = jnp.dot(normed_mid, up_full, preferred_element_type=jnp.float32)
    activated = jax.nn.gelu(up_value).astype(jnp.bfloat16)
    mlp_part = jnp.dot(activated, down_full, preferred_element_type=jnp.float32)
    mlp_share = (
        lax.psum_scatter(
            mlp_part.reshape(strided).astype(jnp.bfloat16),
            "tensor",
            scatter_dimension=2,
            tiled=True,
        )
        .astype(jnp.float32)
        .reshape(-1, model_width)
    )
    branch = attn_share + mlp_share
    out_share = (flat_tokens + gate_value[:, None] * branch).astype(jnp.bfloat16)
    out_all = lax.all_gather(out_share.reshape(mine), "tensor", axis=2, tiled=True).reshape(
        seq_count, routed, model_width
    )
    target = place_target(routed_index, offset, pos_span)
    mixed = place_rows(tokens, out_all, target)
    back_params = (
        lax.all_gather(query_weight, "fsdp", axis=0, tiled=True),
        lax.all_gather(key_weight, "fsdp", axis=0, tiled=True),
        lax.all_gather(value_weight, "fsdp", axis=0, tiled=True),
        lax.all_gather(output_weight, "fsdp", axis=1, tiled=True),
        lax.all_gather(up_weight, "fsdp", axis=0, tiled=True),
        lax.all_gather(down_weight, "fsdp", axis=1, tiled=True),
        lax.all_gather(router_weight, "fsdp", axis=0, tiled=True),
        lax.all_gather(attn_gain, "fsdp", axis=0, tiled=True),
        lax.all_gather(mlp_gain, "fsdp", axis=0, tiled=True),
    )
    (
        query_back,
        key_back,
        value_back,
        output_back,
        up_back,
        down_back,
        router_back,
        first_gain_back,
        second_gain_back,
    ) = back_params
    gate_grad = jnp.sum(grad_flat * branch, axis=-1) * gate_value * (1.0 - gate_value)
    router_part = jnp.sum(flat_tokens * gate_grad[:, None], axis=0)
    branch_grad = gate_value[:, None] * grad_flat
    input_rows_grad = grad_flat + gate_grad[:, None] * router_back.astype(jnp.float32)
    mlp_grad_all = lax.all_gather(
        branch_grad.astype(jnp.bfloat16).reshape(mine), "tensor", axis=2, tiled=True
    ).reshape(-1, model_width)
    down_grad = jnp.einsum("rf,rd->fd", activated, mlp_grad_all, preferred_element_type=jnp.float32)
    act_grad = jnp.einsum("rd,fd->rf", mlp_grad_all, down_back, preferred_element_type=jnp.float32)
    gelu_out, gelu_back = jax.vjp(jax.nn.gelu, up_value)
    up_grad = gelu_back(act_grad)[0].astype(jnp.bfloat16)
    up_grad_weight = jnp.einsum(
        "rd,rf->df", normed_mid, up_grad, preferred_element_type=jnp.float32
    )
    mid_part = jnp.einsum("rf,df->rd", up_grad, up_back, preferred_element_type=jnp.float32)
    mid_share = lax.psum_scatter(
        mid_part.reshape(strided), "tensor", scatter_dimension=2, tiled=True
    ).reshape(-1, model_width)
    hidden_grad, second_gain_grad = norm_back(
        mid_share, hidden_in, second_scale, second_gain_back.astype(jnp.float32)
    )
    input_rows_grad = input_rows_grad + hidden_grad
    attn_grad_rows = (branch_grad + hidden_grad).astype(jnp.bfloat16)
    attn_grad_all = lax.all_gather(
        attn_grad_rows.reshape(mine), "tensor", axis=2, tiled=True
    ).reshape(-1, model_width)
    output_grad_weight = jnp.einsum(
        "rc,rd->cd", context, attn_grad_all, preferred_element_type=jnp.float32
    )
    context_grad = (
        jnp.einsum("rd,cd->rc", attn_grad_all, output_back, preferred_element_type=jnp.float32)
        .astype(jnp.bfloat16)
        .reshape(head_shape)
    )
    scores_again = attend_scores(query_heads, key_heads, allowed, score_scale)
    probs_exact = jnp.exp(scores_again - log_total)
    prob_grad = jnp.einsum(
        "sqhe,skhe->shqk", context_grad, value_heads, preferred_element_type=jnp.float32
    )
    value_grad = jnp.einsum(
        "shqk,sqhe->skhe",
        probs_exact.astype(jnp.bfloat16),
        context_grad,
        preferred_element_type=jnp.float32,
    ).astype(jnp.bfloat16)
    row_inner = jnp.sum(probs_exact * prob_grad, axis=-1, keepdims=True)
    score_grad = (probs_exact * (prob_grad - row_inner)).astype(jnp.bfloat16)
    query_grad = (
        (
            jnp.einsum("shqk,skhe->sqhe", score_grad, key_heads, preferred_element_type=jnp.float32)
            * score_scale
        )
        .astype(jnp.bfloat16)
        .reshape(-1, local_width)
    )
    key_grad = (
        (
            jnp.einsum(
                "shqk,sqhe->skhe", score_grad, query_heads, preferred_element_type=jnp.float32
            )
            * score_scale
        )
        .astype(jnp.bfloat16)
        .reshape(-1, local_width)
    )
    value_grad = value_grad.reshape(-1, local_width)
    query_grad_weight = jnp.einsum(
        "rd,rc->dc", normed_all, query_grad, preferred_element_type=jnp.float32
    )
    key_grad_weight = jnp.einsum(
        "rd,rc->dc", normed_all, key_grad, preferred_element_type=jnp.float32
    )
    value_grad_weight = jnp.einsum(
        "rd,rc->dc", normed_all, value_grad, preferred_element_type=jnp.float32
    )
    first_part = jnp.einsum("rc,dc->rd", query_grad, query_back, preferred_element_type=jnp.float32)
    first_part = first_part + jnp.einsum(
        "rc,dc->rd", key_grad, key_back, preferred_element_type=jnp.float32
    )
    first_part = first_part + jnp.einsum(
        "rc,dc->rd", value_grad, value_back, preferred_element_type=jnp.float32
    )
    first_share = lax.psum_scatter(
        first_part.reshape(strided), "tensor", scatter_dimension=2, tiled=True
    ).reshape(-1, model_width)
    norm_grad, first_gain_grad = norm_back(
        first_share, flat_tokens, first_scale, first_gain_back.astype(jnp.float32)
    )
    input_rows_grad = input_rows_grad + norm_grad
    vector_part = jnp.stack([router_part, first_gain_grad, second_gain_grad])
    rows_back, vector_all = (
        lax.all_gather(input_rows_grad.reshape(mine), "tensor", axis=2, tiled=True),
        lax.all_gather(vector_part, "tensor", axis=0, tiled=True),
    )
    vector_sum = jnp.sum(vector_all.reshape(tensor_count, 3, model_width), axis=0)
    token_grad = place_rows(
        cotangent, rows_back.reshape(seq_count, routed, model_width).astype(jnp.bfloat16), target
    )
    summed = (
        lax.psum_scatter(query_grad_weight, "fsdp", scatter_dimension=0, tiled=True),
        lax.psum_scatter(key_grad_weight, "fsdp", scatter_dimension=0, tiled=True),
        lax.psum_scatter(value_grad_weight, "fsdp", scatter_dimension=0, tiled=True),
        lax.psum_scatter(output_grad_weight, "fsdp", scatter_dimension=1, tiled=True),
        lax.psum_scatter(up_grad_weight, "fsdp", scatter_dimension=0, tiled=True),
        lax.psum_scatter(down_grad, "fsdp", scatter_dimension=1, tiled=True),
        lax.psum_scatter(vector_sum[0], "fsdp", scatter_dimension=0, tiled=True),
        lax.psum_scatter(vector_sum[1], "fsdp", scatter_dimension=0, tiled=True),
        lax.psum_scatter(vector_sum[2], "fsdp", scatter_dimension=0, tiled=True),
    )
    return (
        mixed,
        token_grad,
        summed[0],
        summed[1],
        summed[2],
        summed[3],
        summed[4],
        summed[5],
        summed[6],
        summed[7],
        summed[8],
    )


def solution(mesh):
    in_specs = (
        P("fsdp", "tensor", None),
        P("fsdp", "tensor", None),
        P("fsdp", None),
        P("fsdp", "tensor"),
        P("fsdp", "tensor"),
        P("fsdp", "tensor"),
        P("tensor", "fsdp"),
        P("fsdp", "tensor"),
        P("tensor", "fsdp"),
        P("fsdp"),
        P("fsdp"),
        P("fsdp"),
    )
    out_specs = (
        P("fsdp", "tensor", None),
        P("fsdp", "tensor", None),
        P("fsdp", "tensor"),
        P("fsdp", "tensor"),
        P("fsdp", "tensor"),
        P("tensor", "fsdp"),
        P("fsdp", "tensor"),
        P("tensor", "fsdp"),
        P("fsdp"),
        P("fsdp"),
        P("fsdp"),
    )
    return jax.shard_map(shards, mesh=mesh, in_specs=in_specs, out_specs=out_specs, check_vma=False)
```

profile of v0, /device:TPU:0, one launch (start us, length us, event | category | flops | bytes accessed | tf_op | source)
XLA Modules:
  0.0 1439.0 jit_solution(8234796519459619486)
XLA Ops:
  14.4 39.2 %gather_fusion = bf16[1024,1024]{1,0:T(8,128)(2,1)S(1)} fusion(bf16[8,256,1024]{2,1,0:T(8,128)(2,1)} %copy.187, s32[1024]{0:T(1024)S(1)} %or_bitcast_fusion), kind=kCustom, calls=%fused_computation.clone | custom fusion | bytes 4202496 | tf_op jit(solution)/shard_map/jit(take_along_axis)/gather | solution.py:17
  53.6 44.5 %gather_fusion.1 = bf16[1024,1024]{1,0:T(8,128)(2,1)} fusion(bf16[8,256,1024]{2,1,0:T(8,128)(2,1)} %copy.188, s32[1024]{0:T(1024)S(1)} %or_bitcast_fusion), kind=kCustom, calls=%fused_computation.1.clone | custom fusion | bytes 4202496 | tf_op jit(solution)/shard_map/jit(take_along_axis)/gather | solution.py:17
  110.1 21.4 %all-gather.1 = bf16[8,1,128]{2,1,0:T(2,128)(2,1)S(1)} all-gather(bf16[1,1,128]{2,1,0:T(2,128)(2,1)S(1)} %bitcast.220), channel_id=1, replica_groups=mesh['fsdp'=8,'tensor'=4] {'fsdp'}, dimensions={0}, use_global_device_ids=true | all-gather | bytes 2304 | tf_op jit(solution)/shard_map/all_gather | solution.py:96
  132.1 29.9 %all-reduce.17.cloned.1.call-done = bf16[8,32,4,1024]{3,1,2,0:T(8,128)(2,1)} async-done(((bf16[8,32,4,1024]{3,1,2,0:T(8,128)(2,1)}), bf16[8,32,4,1024]{3,1,2,0:T(8,128)(2,1)}) %all-reduce.17.cloned.1.call-update) | async-done | bytes 2097168
  166.1 31.6 %all_gather.61 = bf16[1024,256]{1,0:T(8,128)(2,1)S(1)} all-gather(bf16[128,256]{1,0:T(8,128)(2,1)S(1)} %copy-done.21), channel_id=1, replica_groups=mesh['fsdp'=8,'tensor'=4] {'fsdp'}, dimensions={0}, use_global_device_ids=true | all-gather | bytes 589824 | tf_op jit(solution)/shard_map/all_gather | solution.py:89
  197.7 31.5 %all_gather.62 = bf16[1024,256]{1,0:T(8,128)(2,1)S(1)} all-gather(bf16[128,256]{1,0:T(8,128)(2,1)S(1)} %copy-done.22), channel_id=1, replica_groups=mesh['fsdp'=8,'tensor'=4] {'fsdp'}, dimensions={0}, use_global_device_ids=true | all-gather | bytes 589824 | tf_op jit(solution)/shard_map/all_gather | solution.py:90
  229.1 33.5 %all_gather.60 = bf16[1024,256]{1,0:T(8,128)(2,1)} all-gather(bf16[128,256]{1,0:T(8,128)(2,1)S(1)} %copy-done.23), channel_id=1, replica_groups=mesh['fsdp'=8,'tensor'=4] {'fsdp'}, dimensions={0}, use_global_device_ids=true | all-gather | bytes 589824 | tf_op jit(solution)/shard_map/all_gather | solution.py:91
  262.6 28.6 %all_gather.63 = bf16[256,1024]{1,0:T(8,128)(2,1)} all-gather(bf16[256,128]{1,0:T(8,128)(2,1)S(1)} %copy-done.24), channel_id=1, replica_groups=mesh['fsdp'=8,'tensor'=4] {'fsdp'}, dimensions={1}, use_global_device_ids=true | all-gather | bytes 589824 | tf_op jit(solution)/shard_map/all_gather | solution.py:92
  317.5 19.0 %all-gather.2 = bf16[8,1,128]{2,1,0:T(2,128)(2,1)S(1)} all-gather(bf16[1,1,128]{2,1,0:T(2,128)(2,1)S(1)} %bitcast.221), channel_id=1, replica_groups=mesh['fsdp'=8,'tensor'=4] {'fsdp'}, dimensions={0}, use_global_device_ids=true | all-gather | bytes 2304 | tf_op jit(solution)/shard_map/all_gather | solution.py:97
  336.4 64.6 %all-reduce.19.cloned.1.call-done = f32[8,32,4,1024]{3,1,2,0:T(8,128)} async-done(((f32[8,32,4,1024]{3,1,2,0:T(8,128)}), f32[8,32,4,1024]{3,1,2,0:T(8,128)}) %all-reduce.19.cloned.1.call-update) | async-done | bytes 4194320
  435.7 42.7 %all-gather.17.cloned.1.call-done = bf16[1024,1024]{1,0:T(8,128)(2,1)} async-done(((bf16[128,1024]{1,0:T(8,128)(2,1)}), bf16[1024,1024]{1,0:T(8,128)(2,1)}) %all-gather.17.cloned.1.call-update) | async-done | bytes 2097168 | tf_op jit(solution)/shard_map/all_gather | solution.py:93
  485.0 45.0 %all-gather.19.cloned.1.call-done = bf16[1024,1024]{1,0:T(8,128)(2,1)} async-done(((bf16[1024,128]{1,0:T(8,128)(2,1)}), bf16[1024,1024]{1,0:T(8,128)(2,1)}) %all-gather.19.cloned.1.call-update) | async-done | bytes 2097168 | tf_op jit(solution)/shard_map/all_gather | solution.py:94
  545.3 17.6 %all-gather = bf16[8,1,128]{2,1,0:T(2,128)(2,1)S(1)} all-gather(bf16[1,1,128]{2,1,0:T(2,128)(2,1)S(1)} %bitcast.222), channel_id=1, replica_groups=mesh['fsdp'=8,'tensor'=4] {'fsdp'}, dimensions={0}, use_global_device_ids=true | all-gather | bytes 2304 | tf_op jit(solution)/shard_map/all_gather | solution.py:95
  564.1 64.5 %all-reduce.25.cloned.1.call-done = (bf16[8,32,4,1024]{3,1,2,0:T(8,128)(2,1)}, bf16[8,32,4,1024]{3,1,2,0:T(8,128)(2,1)}) async-done(((bf16[8,32,4,1024]{3,1,2,0:T(8,128)(2,1)}, bf16[8,32,4,1024]{3,1,2,0:T(8,128)(2,1)}), (bf16[8,32,4,1024]{3,1,2,0:T(8,128)(2,1)}, bf16[8,32,4,1024]{3,1,2,0:T(8,128)(2,1)})) %all-reduce.25.cloned.1.call-update) | async-done | bytes 4194320
  634.2 22.6 %all-gather.23.cloned.1.call-done = bf16[8,32,4,1024]{3,1,2,0:T(8,128)(2,1)} async-done(((bf16[8,32,1,1024]{3,1,2,0:T(8,128)(2,1)}), bf16[8,32,4,1024]{3,1,2,0:T(8,128)(2,1)}) %all-gather.23.cloned.1.call-update) | async-done | bytes 2097168 | tf_op jit(solution)/shard_map/all_gather | solution.py:203
  690.9 85.6 %all-reduce.21.cloned.1.call-done = f32[8,32,4,1024]{3,1,2,0:T(8,128)} async-done(((f32[8,32,4,1024]{3,1,2,0:T(8,128)}), f32[8,32,4,1024]{3,1,2,0:T(8,128)}) %all-reduce.21.cloned.1.call-update) | async-done | bytes 4194320
  782.4 22.4 %all-gather.25.cloned.1.call-done = bf16[8,32,4,1024]{3,1,2,0:T(8,128)(2,1)} async-done(((bf16[8,32,1,1024]{3,1,2,0:T(8,128)(2,1)}), bf16[8,32,4,1024]{3,1,2,0:T(8,128)(2,1)}) %all-gather.25.cloned.1.call-update) | async-done | bytes 2097168 | tf_op jit(solution)/shard_map/all_gather | solution.py:222
  844.4 85.5 %all-reduce.23.cloned.1.call-done = f32[8,32,4,1024]{3,1,2,0:T(8,128)} async-done(((f32[8,32,4,1024]{3,1,2,0:T(8,128)}), f32[8,32,4,1024]{3,1,2,0:T(8,128)}) %all-reduce.23.cloned.1.call-update) | async-done | bytes 4194320
  971.2 37.5 %all-reduce.9 = (f32[1024]{0:T(1024)S(1)}, f32[1024]{0:T(1024)S(1)}, f32[1024]{0:T(1024)S(1)}) all-reduce(f32[1024]{0:T(1024)S(1)} %bitcast.218, f32[1024]{0:T(1024)S(1)} %bitcast.217, f32[1024]{0:T(1024)S(1)} %bitcast.216), channel_id=14, replica_groups=mesh['fsdp'=8,'tensor'=4] {'fsdp'}, use_global_device_ids=true, to_apply=%region_26.28.clone | all-reduce | flops 3072 | bytes 24576
  1049.2 66.4 %reduce-scatter.29.cloned.1.call-done = f32[128,256]{1,0:T(8,128)} async-done(((f32[1024,256]{1,0:T(8,128)}), f32[128,256]{1,0:T(8,128)}) %reduce-scatter.29.cloned.1.call-update) | async-done | bytes 131088 | tf_op jit(solution)/shard_map/reduce_scatter | solution.py:300
  1115.6 66.7 %reduce-scatter.25.cloned.1.call-done = f32[128,256]{1,0:T(8,128)} async-done(((f32[1024,256]{1,0:T(8,128)}), f32[128,256]{1,0:T(8,128)}) %reduce-scatter.25.cloned.1.call-update) | async-done | bytes 131088 | tf_op jit(solution)/shard_map/reduce_scatter | solution.py:298
  1182.3 66.1 %reduce-scatter.27.cloned.1.call-done = f32[128,256]{1,0:T(8,128)} async-done(((f32[1024,256]{1,0:T(8,128)}), f32[128,256]{1,0:T(8,128)}) %reduce-scatter.27.cloned.1.call-update) | async-done | bytes 131088 | tf_op jit(solution)/shard_map/reduce_scatter | solution.py:299
  1248.5 91.9 %reduce-scatter.35.cloned.1.call-done = f32[1024,128]{1,0:T(8,128)} async-done(((f32[1024,1024]{1,0:T(8,128)}), f32[1024,128]{1,0:T(8,128)}) %reduce-scatter.35.cloned.1.call-update) | async-done | bytes 524304 | tf_op jit(solution)/shard_map/reduce_scatter | solution.py:303
  1340.3 91.9 %reduce-scatter.33.cloned.1.call-done = f32[128,1024]{1,0:T(8,128)} async-done(((f32[1024,1024]{1,0:T(8,128)}), f32[128,1024]{1,0:T(8,128)}) %reduce-scatter.33.cloned.1.call-update) | async-done | bytes 524304 | tf_op jit(solution)/shard_map/reduce_scatter | solution.py:302
  (222 shorter events, 273.3 us)
Async XLA Ops:
  7.2 154.9 %all-reduce.17.cloned.1.call-start = ((), (), s32[]{:S(2)}) async-start(), calls=%async_computation.20 | async-start | bytes 4194304
  109.5 88.2 %copy-start.22 = (bf16[128,256]{1,0:T(8,128)(2,1)S(1)}, bf16[128,256]{1,0:T(8,128)(2,1)}, u32[]{:S(2)}) copy-start(bf16[128,256]{1,0:T(8,128)(2,1)} %param.18) | copy-start | bytes 196612
  109.5 119.6 %copy-start.23 = (bf16[128,256]{1,0:T(8,128)(2,1)S(1)}, bf16[128,256]{1,0:T(8,128)(2,1)}, u32[]{:S(2)}) copy-start(bf16[128,256]{1,0:T(8,128)(2,1)} %param.19) | copy-start | bytes 196612
  109.5 181.7 %all-gather.13.cloned.1.call-start = ((), (), s32[]{:S(2)}) async-start(), calls=%async_computation.6 | async-start | bytes 2621440 | tf_op jit(solution)/shard_map/all_gather | solution.py:114
  162.1 100.5 %copy-start.24 = (bf16[256,128]{1,0:T(8,128)(2,1)S(1)}, bf16[256,128]{1,0:T(8,128)(2,1)}, u32[]{:S(2)}) copy-start(bf16[256,128]{1,0:T(8,128)(2,1)} %param.20) | copy-start | bytes 196612
  165.8 235.3 %all-reduce.19.cloned.1.call-start = ((), (), s32[]{:S(2)}) async-start(), calls=%async_computation.21 | async-start | bytes 8388608
  197.7 102.1 %copy-start.14 = (bf16[1024,256]{1,0:T(8,128)(2,1)}, bf16[1024,256]{1,0:T(8,128)(2,1)S(1)}, u32[]{:S(2)}) copy-start(bf16[1024,256]{1,0:T(8,128)(2,1)S(1)} %all_gather.61) | copy-start | bytes 1572868
  316.8 110.4 %all-gather.15.cloned.1.call-start = ((), (), s32[]{:S(2)}) async-start(), calls=%async_computation.7 | async-start | bytes 2621440 | tf_op jit(solution)/shard_map/all_gather | solution.py:154
  404.3 74.2 %all-gather.17.cloned.1.call-start = ((), (), s32[]{:S(2)}) async-start(), calls=%async_computation.8 | async-start | bytes 2359296 | tf_op jit(solution)/shard_map/all_gather | solution.py:93
  404.9 125.1 %all-gather.19.cloned.1.call-start = ((), (), s32[]{:S(2)}) async-start(), calls=%async_computation.9 | async-start | bytes 2359296 | tf_op jit(solution)/shard_map/all_gather | solution.py:94
  405.5 223.2 %all-reduce.25.cloned.1.call-start = ((), (), s32[]{:S(2)}) async-start(), calls=%async_computation.24 | async-start | bytes 8388608
  544.7 112.2 %all-gather.23.cloned.1.call-start = ((), (), s32[]{:S(2)}) async-start(), calls=%async_computation.11 | async-start | bytes 2621440 | tf_op jit(solution)/shard_map/all_gather | solution.py:203
  633.9 142.6 %all-reduce.21.cloned.1.call-start = ((), (), s32[]{:S(2)}) async-start(), calls=%async_computation.22 | async-start | bytes 8388608
  690.9 114.0 %all-gather.25.cloned.1.call-start = ((), (), s32[]{:S(2)}) async-start(), calls=%async_computation.12 | async-start | bytes 2621440 | tf_op jit(solution)/shard_map/all_gather | solution.py:222
  782.0 147.9 %all-reduce.23.cloned.1.call-start = ((), (), s32[]{:S(2)}) async-start(), calls=%async_computation.23 | async-start | bytes 8388608
  844.2 85.7 %copy-start.1 = (bf16[8,32,1,1024]{3,1,2,0:T(8,128)(2,1)S(1)}, bf16[8,32,1,1024]{3,1,2,0:T(8,128)(2,1)}, u32[]{:S(2)}) copy-start(bf16[8,32,1,1024]{3,1,2,0:T(8,128)(2,1)} %copy-done) | copy-start | bytes 1572868
  844.2 166.2 %all-gather.21.cloned.1.call-start = ((), (), s32[]{:S(2)}) async-start(), calls=%async_computation.10 | async-start | bytes 2621440 | tf_op jit(solution)/shard_map/all_gather | solution.py:172
  933.6 84.0 %all-gather.27.cloned.1.call-start = ((), (), s32[]{:S(2)}) async-start(), calls=%async_computation.13 | async-start | bytes 2621440 | tf_op jit(solution)/shard_map/all_gather | solution.py:290
  937.8 111.4 %reduce-scatter.31.cloned.1.call-start = ((), (), s32[]{:S(2)}) async-start(), calls=%async_computation.17 | async-start | bytes 1179648 | tf_op jit(solution)/shard_map/reduce_scatter | solution.py:301
  941.7 173.8 %reduce-scatter.29.cloned.1.call-start = ((), (), s32[]{:S(2)}) async-start(), calls=%async_computation.16 | async-start | bytes 1179648 | tf_op jit(solution)/shard_map/reduce_scatter | solution.py:300
  944.7 237.7 %reduce-scatter.25.cloned.1.call-start = ((), (), s32[]{:S(2)}) async-start(), calls=%async_computation.14 | async-start | bytes 1179648 | tf_op jit(solution)/shard_map/reduce_scatter | solution.py:298
  946.5 302.0 %reduce-scatter.27.cloned.1.call-start = ((), (), s32[]{:S(2)}) async-start(), calls=%async_computation.15 | async-start | bytes 1179648 | tf_op jit(solution)/shard_map/reduce_scatter | solution.py:299
  948.3 392.0 %reduce-scatter.35.cloned.1.call-start = ((), (), s32[]{:S(2)}) async-start(), calls=%async_computation.19 | async-start | bytes 4718592 | tf_op jit(solution)/shard_map/reduce_scatter | solution.py:303
  956.0 476.1 %reduce-scatter.33.cloned.1.call-start = ((), (), s32[]{:S(2)}) async-start(), calls=%async_computation.18 | async-start | bytes 4718592 | tf_op jit(solution)/shard_map/reduce_scatter | solution.py:302
  (30 other events, 213.5 us)
Sparse Core Ops, SparseCore 0:
  109.6 52.3 all-reduce.16
  165.9 22.6 all-gather.12
  316.9 84.0 all-reduce.18
  404.4 22.7 all-gather.14
  429.2 49.2 all-gather.16
  480.4 49.5 all-gather.18
  544.8 83.8 all-reduce.24
  634.1 22.7 all-gather.22
  691.0 85.4 all-reduce.20
  782.1 22.7 all-gather.24
  844.4 85.4 all-reduce.22
  933.8 22.7 all-gather.20
  958.2 22.9 all-gather.26
  985.3 63.8 reduce-scatter.30
  1053.0 62.4 reduce-scatter.28
  1119.8 62.4 reduce-scatter.24
  1186.1 62.2 reduce-scatter.26
  1253.0 87.3 reduce-scatter.34
  1344.5 87.6 reduce-scatter.32
where the time goes:
time: 1450 us; the launch traced here: 1440 us
  waiting for transfers between devices  866 us (60%)
  blocking collectives  226 us (16%)
  local copies, waits for them, and re-layouts  221 us (15%)
  matrix products  74.1 us (5%)
  other arithmetic  34.6 us (2%)
  between operations  15.4 us (1%)
    unnamed x24, waiting for transfers between devices  332 us
    reduce_scatter x1, waiting for transfers between devices, shards(): lax.psum_scatter(up_grad_weight, 'fsdp', scatter_dimension=0, tiled=True)  91.9 us
    reduce_scatter x1, waiting for transfers between devices, shards(): lax.psum_scatter(down_grad, 'fsdp', scatter_dimension=1, tiled=True)  91.9 us
    gather x2, local copies, waits for them, and re-layouts, pick_rows(): jnp.take_along_axis(values, safe_pos[:, :, None], axis=1)  83.7 us
    reduce_scatter x1, waiting for transfers between devices, shards(): lax.psum_scatter(query_grad_weight, 'fsdp', scatter_dimension=0, tiled=True)  66.7 us
    reduce_scatter x1, waiting for transfers between devices, shards(): lax.psum_scatter(value_grad_weight, 'fsdp', scatter_dimension=0, tiled=True)  66.4 us
    reduce_scatter x1, waiting for transfers between devices, shards(): lax.psum_scatter(key_grad_weight, 'fsdp', scatter_dimension=0, tiled=True)  66.1 us
    all_gather x1, waiting for transfers between devices, shards(): lax.all_gather(down_weight, 'fsdp', axis=1, tiled=True)  45 us
  transfers between devices with their start and end apart: 19, of which 16 were waited for; matrix products, arithmetic and copies ran while one was open for 6% of the time, Pallas kernels for 0%

commit v1 on v0

--- a/solution.py
+++ b/solution.py
@@ -8,6 +8,18 @@
 EPS = 1e-06
 NEG = -1e30
 HIGH = lax.Precision.HIGHEST
+
+
+def collect(shard, axis, dim):
+    ways, here = (lax.axis_size(axis), lax.axis_index(axis))
+    grown, reach = (shard, 1)
+    while reach < ways:
+        theirs = lax.ppermute(grown, axis, [(d, d ^ reach) for d in range(ways)])
+        mine_first = jnp.concatenate([grown, theirs], axis=dim)
+        theirs_first = jnp.concatenate([theirs, grown], axis=dim)
+        grown = jnp.where(here & reach == 0, mine_first, theirs_first)
+        reach = 2 * reach
+    return grown
 
 
 def pick_rows(values, routed_index, offset, pos_span):
@@ -88,7 +100,7 @@
     full_params = (
         lax.all_gather(query_weight, "fsdp", axis=0, tiled=True),
         lax.all_gather(key_weight, "fsdp", axis=0, tiled=True),
-        lax.all_gather(value_weight, "fsdp", axis=0, tiled=True),
+        collect(value_weight, "fsdp", 0),
         lax.all_gather(output_weight, "fsdp", axis=1, tiled=True),
         lax.all_gather(up_weight, "fsdp", axis=0, tiled=True),
         lax.all_gather(down_weight, "fsdp", axis=1, tiled=True),

time: 1450 us -> 1440 us (level)
  waiting for transfers between devices: 866 us -> 851 us
    all_gather x1, waiting for transfers between devices: 22.4 us -> 0.01 us  [shards(): lax.all_gather(attn_grad_rows.reshape(mine), 'tensor', axis=2, tiled=True)]
    unnamed x79 -> x77, local copies, waits for them, and re-layouts: 38.3 us -> 38.2 us
  transfers between devices with their start and end apart: 19 -> 22, of which waited for: 16 -> 16; matrix products, arithmetic and copies ran while one was open for 6% -> 7% of each run, Pallas kernels for 0% -> 0%
where the time goes in v1:
time: 1440 us; the launch traced here: 1430 us
  waiting for transfers between devices  851 us (59%)
  blocking collectives  229 us (16%)
  local copies, waits for them, and re-layouts  220 us (15%)
  matrix products  75.3 us (5%)
  other arithmetic  34.7 us (2%)
  between operations  15.5 us (1%)
    unnamed x24, waiting for transfers between devices  333 us
    reduce_scatter x1, waiting for transfers between devices, shards(): lax.psum_scatter(up_grad_weight, 'fsdp', scatter_dimension=0, tiled=True)  91.9 us
    reduce_scatter x1, waiting for transfers between devices, shards(): lax.psum_scatter(down_grad, 'fsdp', scatter_dimension=1, tiled=True)  91.9 us
    gather x2, local copies, waits for them, and re-layouts, pick_rows(): jnp.take_along_axis(values, safe_pos[:, :, None], axis=1)  83.5 us
    reduce_scatter x1, waiting for transfers between devices, shards(): lax.psum_scatter(query_grad_weight, 'fsdp', scatter_dimension=0, tiled=True)  66.8 us
    reduce_scatter x1, waiting for transfers between devices, shards(): lax.psum_scatter(value_grad_weight, 'fsdp', scatter_dimension=0, tiled=True)  66.3 us
    reduce_scatter x1, waiting for transfers between devices, shards(): lax.psum_scatter(key_grad_weight, 'fsdp', scatter_dimension=0, tiled=True)  66.2 us
    all_gather x1, waiting for transfers between devices, shards(): lax.all_gather(down_weight, 'fsdp', axis=1, tiled=True)  45 us
  transfers between devices with their start and end apart: 22, of which 16 were waited for; matrix products, arithmetic and copies ran while one was open for 7% of the time, Pallas kernels for 0%

profile of v1, /device:TPU:0, one launch (start us, length us, event | category | flops | bytes accessed | tf_op | source)
XLA Modules:
  0.0 1428.6 jit_solution(14199716306647410165)
XLA Ops:
  14.4 39.1 %gather_fusion = bf16[1024,1024]{1,0:T(8,128)(2,1)S(1)} fusion(bf16[8,256,1024]{2,1,0:T(8,128)(2,1)} %copy.187, s32[1024]{0:T(1024)S(1)} %or_bitcast_fusion), kind=kCustom, calls=%fused_computation.clone | custom fusion | bytes 4202496 | tf_op jit(solution)/shard_map/jit(take_along_axis)/gather | solution.py:29
  53.5 44.4 %gather_fusion.1 = bf16[1024,1024]{1,0:T(8,128)(2,1)} fusion(bf16[8,256,1024]{2,1,0:T(8,128)(2,1)} %copy.188, s32[1024]{0:T(1024)S(1)} %or_bitcast_fusion), kind=kCustom, calls=%fused_computation.1.clone | custom fusion | bytes 4202496 | tf_op jit(solution)/shard_map/jit(take_along_axis)/gather | solution.py:29
  110.0 21.5 %all-gather.1 = bf16[8,1,128]{2,1,0:T(2,128)(2,1)S(1)} all-gather(bf16[1,1,128]{2,1,0:T(2,128)(2,1)S(1)} %bitcast.219), channel_id=1, replica_groups=mesh['fsdp'=8,'tensor'=4] {'fsdp'}, dimensions={0}, use_global_device_ids=true | all-gather | bytes 2304 | tf_op jit(solution)/shard_map/all_gather | solution.py:108
  132.0 29.9 %all-reduce.17.cloned.1.call-done = bf16[8,32,4,1024]{3,1,2,0:T(8,128)(2,1)} async-done(((bf16[8,32,4,1024]{3,1,2,0:T(8,128)(2,1)}), bf16[8,32,4,1024]{3,1,2,0:T(8,128)(2,1)}) %all-reduce.17.cloned.1.call-update) | async-done | bytes 2097168
  167.3 31.6 %all_gather.59 = bf16[1024,256]{1,0:T(8,128)(2,1)S(1)} all-gather(bf16[128,256]{1,0:T(8,128)(2,1)S(1)} %copy-done.21), channel_id=1, replica_groups=mesh['fsdp'=8,'tensor'=4] {'fsdp'}, dimensions={0}, use_global_device_ids=true | all-gather | bytes 589824 | tf_op jit(solution)/shard_map/all_gather | solution.py:101
  198.8 31.9 %all_gather.60 = bf16[1024,256]{1,0:T(8,128)(2,1)S(1)} all-gather(bf16[128,256]{1,0:T(8,128)(2,1)S(1)} %copy-done.22), channel_id=1, replica_groups=mesh['fsdp'=8,'tensor'=4] {'fsdp'}, dimensions={0}, use_global_device_ids=true | all-gather | bytes 589824 | tf_op jit(solution)/shard_map/all_gather | solution.py:102
  236.2 33.6 %all_gather.61 = bf16[256,1024]{1,0:T(8,128)(2,1)} all-gather(bf16[256,128]{1,0:T(8,128)(2,1)S(1)} %copy-done.23), channel_id=1, replica_groups=mesh['fsdp'=8,'tensor'=4] {'fsdp'}, dimensions={1}, use_global_device_ids=true | all-gather | bytes 589824 | tf_op jit(solution)/shard_map/all_gather | solution.py:104
  297.0 16.1 %all-gather.2 = bf16[8,1,128]{2,1,0:T(2,128)(2,1)S(1)} all-gather(bf16[1,1,128]{2,1,0:T(2,128)(2,1)S(1)} %bitcast.220), channel_id=1, replica_groups=mesh['fsdp'=8,'tensor'=4] {'fsdp'}, dimensions={0}, use_global_device_ids=true | all-gather | bytes 2304 | tf_op jit(solution)/shard_map/all_gather | solution.py:109
  313.2 66.1 %all-reduce.19.cloned.1.call-done = f32[8,32,4,1024]{3,1,2,0:T(8,128)} async-done(((f32[8,32,4,1024]{3,1,2,0:T(8,128)}), f32[8,32,4,1024]{3,1,2,0:T(8,128)}) %all-reduce.19.cloned.1.call-update) | async-done | bytes 4194320
  388.0 17.4 %all-gather.15.cloned.1.call-done = bf16[8,32,4,1024]{3,1,2,0:T(8,128)(2,1)} async-done(((bf16[8,32,1,1024]{3,1,2,0:T(8,128)(2,1)}), bf16[8,32,4,1024]{3,1,2,0:T(8,128)(2,1)}) %all-gather.15.cloned.1.call-update) | async-done | bytes 2097168 | tf_op jit(solution)/shard_map/all_gather | solution.py:166
  414.0 42.7 %all-gather.17.cloned.1.call-done = bf16[1024,1024]{1,0:T(8,128)(2,1)} async-done(((bf16[128,1024]{1,0:T(8,128)(2,1)}), bf16[1024,1024]{1,0:T(8,128)(2,1)}) %all-gather.17.cloned.1.call-update) | async-done | bytes 2097168 | tf_op jit(solution)/shard_map/all_gather | solution.py:105
  463.1 45.0 %all-gather.19.cloned.1.call-done = bf16[1024,1024]{1,0:T(8,128)(2,1)} async-done(((bf16[1024,128]{1,0:T(8,128)(2,1)}), bf16[1024,1024]{1,0:T(8,128)(2,1)}) %all-gather.19.cloned.1.call-update) | async-done | bytes 2097168 | tf_op jit(solution)/shard_map/all_gather | solution.py:106
  523.6 17.6 %all-gather = bf16[8,1,128]{2,1,0:T(2,128)(2,1)S(1)} all-gather(bf16[1,1,128]{2,1,0:T(2,128)(2,1)S(1)} %bitcast.221), channel_id=1, replica_groups=mesh['fsdp'=8,'tensor'=4] {'fsdp'}, dimensions={0}, use_global_device_ids=true | all-gather | bytes 2304 | tf_op jit(solution)/shard_map/all_gather | solution.py:107
  542.4 64.5 %all-reduce.25.cloned.1.call-done = (bf16[8,32,4,1024]{3,1,2,0:T(8,128)(2,1)}, bf16[8,32,4,1024]{3,1,2,0:T(8,128)(2,1)}) async-done(((bf16[8,32,4,1024]{3,1,2,0:T(8,128)(2,1)}, bf16[8,32,4,1024]{3,1,2,0:T(8,128)(2,1)}), (bf16[8,32,4,1024]{3,1,2,0:T(8,128)(2,1)}, bf16[8,32,4,1024]{3,1,2,0:T(8,128)(2,1)})) %all-reduce.25.cloned.1.call-update) | async-done | bytes 4194320
  612.5 22.6 %all-gather.23.cloned.1.call-done = bf16[8,32,4,1024]{3,1,2,0:T(8,128)(2,1)} async-done(((bf16[8,32,1,1024]{3,1,2,0:T(8,128)(2,1)}), bf16[8,32,4,1024]{3,1,2,0:T(8,128)(2,1)}) %all-gather.23.cloned.1.call-update) | async-done | bytes 2097168 | tf_op jit(solution)/shard_map/all_gather | solution.py:215
  669.2 85.6 %all-reduce.21.cloned.1.call-done = f32[8,32,4,1024]{3,1,2,0:T(8,128)} async-done(((f32[8,32,4,1024]{3,1,2,0:T(8,128)}), f32[8,32,4,1024]{3,1,2,0:T(8,128)}) %all-reduce.21.cloned.1.call-update) | async-done | bytes 4194320
  760.3 33.8 %all_gather.69 = bf16[1024,256]{1,0:T(8,128)(2,1)} all-gather(bf16[128,256]{1,0:T(8,128)(2,1)S(1)} %copy-done.20), channel_id=1, replica_groups=mesh['fsdp'=8,'tensor'=4] {'fsdp'}, dimensions={0}, use_global_device_ids=true | all-gather | bytes 589824 | tf_op jit(solution)/shard_map/all_gather | solution.py:192
  833.7 85.7 %all-reduce.23.cloned.1.call-done = f32[8,32,4,1024]{3,1,2,0:T(8,128)} async-done(((f32[8,32,4,1024]{3,1,2,0:T(8,128)}), f32[8,32,4,1024]{3,1,2,0:T(8,128)}) %all-reduce.23.cloned.1.call-update) | async-done | bytes 4194320
  960.7 37.5 %all-reduce.9 = (f32[1024]{0:T(1024)S(1)}, f32[1024]{0:T(1024)S(1)}, f32[1024]{0:T(1024)S(1)}) all-reduce(f32[1024]{0:T(1024)S(1)} %bitcast.217, f32[1024]{0:T(1024)S(1)} %bitcast.216, f32[1024]{0:T(1024)S(1)} %bitcast.215), channel_id=14, replica_groups=mesh['fsdp'=8,'tensor'=4] {'fsdp'}, use_global_device_ids=true, to_apply=%region_26.28.clone | all-reduce | flops 3072 | bytes 24576
  1038.7 66.3 %reduce-scatter.29.cloned.1.call-done = f32[128,256]{1,0:T(8,128)} async-done(((f32[1024,256]{1,0:T(8,128)}), f32[128,256]{1,0:T(8,128)}) %reduce-scatter.29.cloned.1.call-update) | async-done | bytes 131088 | tf_op jit(solution)/shard_map/reduce_scatter | solution.py:312
  1105.0 66.8 %reduce-scatter.25.cloned.1.call-done = f32[128,256]{1,0:T(8,128)} async-done(((f32[1024,256]{1,0:T(8,128)}), f32[128,256]{1,0:T(8,128)}) %reduce-scatter.25.cloned.1.call-update) | async-done | bytes 131088 | tf_op jit(solution)/shard_map/reduce_scatter | solution.py:310
  1171.8 66.2 %reduce-scatter.27.cloned.1.call-done = f32[128,256]{1,0:T(8,128)} async-done(((f32[1024,256]{1,0:T(8,128)}), f32[128,256]{1,0:T(8,128)}) %reduce-scatter.27.cloned.1.call-update) | async-done | bytes 131088 | tf_op jit(solution)/shard_map/reduce_scatter | solution.py:311
  1238.0 91.9 %reduce-scatter.35.cloned.1.call-done = f32[1024,128]{1,0:T(8,128)} async-done(((f32[1024,1024]{1,0:T(8,128)}), f32[1024,128]{1,0:T(8,128)}) %reduce-scatter.35.cloned.1.call-update) | async-done | bytes 524304 | tf_op jit(solution)/shard_map/reduce_scatter | solution.py:315
  1329.9 91.9 %reduce-scatter.33.cloned.1.call-done = f32[128,1024]{1,0:T(8,128)} async-done(((f32[1024,1024]{1,0:T(8,128)}), f32[128,1024]{1,0:T(8,128)}) %reduce-scatter.33.cloned.1.call-update) | async-done | bytes 524304 | tf_op jit(solution)/shard_map/reduce_scatter | solution.py:314
  (228 shorter events, 263.4 us)
Async XLA Ops:
  7.2 154.8 %all-reduce.17.cloned.1.call-start = ((), (), s32[]{:S(2)}) async-start(), calls=%async_computation.20 | async-start | bytes 4194304
  109.3 89.5 %copy-start.22 = (bf16[128,256]{1,0:T(8,128)(2,1)S(1)}, bf16[128,256]{1,0:T(8,128)(2,1)}, u32[]{:S(2)}) copy-start(bf16[128,256]{1,0:T(8,128)(2,1)} %param.18) | copy-start | bytes 196612
  109.3 160.5 %all-gather.13.cloned.1.call-start = ((), (), s32[]{:S(2)}) async-start(), calls=%async_computation.6 | async-start | bytes 2621440 | tf_op jit(solution)/shard_map/all_gather | solution.py:126
  165.7 213.6 %all-reduce.19.cloned.1.call-start = ((), (), s32[]{:S(2)}) async-start(), calls=%async_computation.21 | async-start | bytes 8388608
  165.7 65.0 %collective-permute-start = (bf16[128,256]{1,0:T(8,128)(2,1)S(1)}, bf16[128,256]{1,0:T(8,128)(2,1)S(1)}, u32[]{:S(2)}, u32[]{:S(2)}) collective-permute-start(bf16[128,256]{1,0:T(8,128)(2,1)S(1)} %copy-done.19), channel_id=1, source_target_pairs={{0,4},{4,0},{8,12},{12,8},{16,20},{20,16},{24,28},{28,24},{1,5},{5... | collective-permute-start | bytes 196616 | tf_op jit(solution)/shard_map/ppermute | solution.py:17
  230.8 5.0 collective-permute-start.1
  235.9 39.2 %collective-permute-start.2 = (bf16[512,256]{1,0:T(8,128)(2,1)S(1)}, bf16[512,256]{1,0:T(8,128)(2,1)}, u32[]{:S(2)}, u32[]{:S(2)}) collective-permute-start(bf16[512,256]{1,0:T(8,128)(2,1)S(1)} %maximum_select_fusion.2), channel_id=1, source_target_pairs={{0,16},{4,20},{8,24},{12,28},{16,0},{20,4},{24,8},{28,12},{1,17},{... | collective-permute-start | bytes 786440 | tf_op jit(solution)/shard_map/ppermute | solution.py:17
  296.4 108.9 %all-gather.15.cloned.1.call-start = ((), (), s32[]{:S(2)}) async-start(), calls=%async_computation.7 | async-start | bytes 2621440 | tf_op jit(solution)/shard_map/all_gather | solution.py:166
  382.5 74.2 %all-gather.17.cloned.1.call-start = ((), (), s32[]{:S(2)}) async-start(), calls=%async_computation.8 | async-start | bytes 2359296 | tf_op jit(solution)/shard_map/all_gather | solution.py:105
  383.0 125.1 %all-gather.19.cloned.1.call-start = ((), (), s32[]{:S(2)}) async-start(), calls=%async_computation.9 | async-start | bytes 2359296 | tf_op jit(solution)/shard_map/all_gather | solution.py:106
  383.6 223.3 %all-reduce.25.cloned.1.call-start = ((), (), s32[]{:S(2)}) async-start(), calls=%async_computation.24 | async-start | bytes 8388608
  522.9 112.1 %all-gather.23.cloned.1.call-start = ((), (), s32[]{:S(2)}) async-start(), calls=%async_computation.11 | async-start | bytes 2621440 | tf_op jit(solution)/shard_map/all_gather | solution.py:215
  612.2 142.6 %all-reduce.21.cloned.1.call-start = ((), (), s32[]{:S(2)}) async-start(), calls=%async_computation.22 | async-start | bytes 8388608
  669.1 125.0 %all-gather.25.cloned.1.call-start = ((), (), s32[]{:S(2)}) async-start(), calls=%async_computation.12 | async-start | bytes 2621440 | tf_op jit(solution)/shard_map/all_gather | solution.py:234
  760.3 159.1 %all-reduce.23.cloned.1.call-start = ((), (), s32[]{:S(2)}) async-start(), calls=%async_computation.23 | async-start | bytes 8388608
  833.5 85.9 %copy-start.1 = (bf16[8,32,1,1024]{3,1,2,0:T(8,128)(2,1)S(1)}, bf16[8,32,1,1024]{3,1,2,0:T(8,128)(2,1)}, u32[]{:S(2)}) copy-start(bf16[8,32,1,1024]{3,1,2,0:T(8,128)(2,1)} %copy-done) | copy-start | bytes 1572868
  833.5 166.4 %all-gather.21.cloned.1.call-start = ((), (), s32[]{:S(2)}) async-start(), calls=%async_computation.10 | async-start | bytes 2621440 | tf_op jit(solution)/shard_map/all_gather | solution.py:184
  923.1 84.0 %all-gather.27.cloned.1.call-start = ((), (), s32[]{:S(2)}) async-start(), calls=%async_computation.13 | async-start | bytes 2621440 | tf_op jit(solution)/shard_map/all_gather | solution.py:302
  927.3 111.4 %reduce-scatter.31.cloned.1.call-start = ((), (), s32[]{:S(2)}) async-start(), calls=%async_computation.17 | async-start | bytes 1179648 | tf_op jit(solution)/shard_map/reduce_scatter | solution.py:313
  931.3 173.8 %reduce-scatter.29.cloned.1.call-start = ((), (), s32[]{:S(2)}) async-start(), calls=%async_computation.16 | async-start | bytes 1179648 | tf_op jit(solution)/shard_map/reduce_scatter | solution.py:312
  934.2 237.6 %reduce-scatter.25.cloned.1.call-start = ((), (), s32[]{:S(2)}) async-start(), calls=%async_computation.14 | async-start | bytes 1179648 | tf_op jit(solution)/shard_map/reduce_scatter | solution.py:310
  936.0 302.0 %reduce-scatter.27.cloned.1.call-start = ((), (), s32[]{:S(2)}) async-start(), calls=%async_computation.15 | async-start | bytes 1179648 | tf_op jit(solution)/shard_map/reduce_scatter | solution.py:311
  937.8 392.1 %reduce-scatter.35.cloned.1.call-start = ((), (), s32[]{:S(2)}) async-start(), calls=%async_computation.19 | async-start | bytes 4718592 | tf_op jit(solution)/shard_map/reduce_scatter | solution.py:315
  945.6 476.2 %reduce-scatter.33.cloned.1.call-start = ((), (), s32[]{:S(2)}) async-start(), calls=%async_computation.18 | async-start | bytes 4718592 | tf_op jit(solution)/shard_map/reduce_scatter | solution.py:314
  (32 other events, 410.5 us)
Sparse Core Ops, SparseCore 0:
  109.5 52.4 all-reduce.16
  165.8 22.6 all-gather.12
  296.5 82.6 all-reduce.18
  382.6 22.7 all-gather.14
  407.3 49.2 all-gather.16
  458.5 49.5 all-gather.18
  523.1 83.8 all-reduce.24
  612.3 22.7 all-gather.22
  669.3 85.4 all-reduce.20
  760.4 22.7 all-gather.24
  833.6 85.6 all-reduce.22
  923.3 22.7 all-gather.20
  947.7 22.9 all-gather.26
  974.9 63.8 reduce-scatter.30
  1042.5 62.4 reduce-scatter.28
  1109.3 62.5 reduce-scatter.24
  1175.6 62.3 reduce-scatter.26
  1242.5 87.3 reduce-scatter.34
  1334.1 87.6 reduce-scatter.32
